TPU v7x, 32 devices: a whole 2x2x4 slice. The times are simulated.
32 devices in a mesh: ctx: 16 (over z, x, core), head: 2 (over y).
Axes of the slice: x: 2, y: 2, z: 4, core: 2. Of those that a mesh axis runs over, the one named last changes fastest.
Arguments:
- query_rows: bfloat16 [8192, 2048], P('ctx', 'head'), may hold values from -60 to 60
- key_rows: bfloat16 [8192, 2048], P('ctx', 'head'), may hold values from -6 to 6
- value_rows: bfloat16 [8192, 2048], P('ctx', 'head'), may hold values from -60 to 60
- log_gate: float32 [16, 8192], P('head', 'ctx'), may hold values from -0.5 to 0
- conv_weight: float32 [3, 4, 2048], P(None, None, 'head'), may hold values from -3 to 3
- norm_gain: float32 [2048], P('head'), may hold values from 0.5 to 1.5
- mixed_grad: bfloat16 [8192, 2048], P('ctx', 'head'), may hold values from -24 to 24
Outputs:
- mixer_out: bfloat16 [8192, 2048], P('ctx', 'head')
- query_grad: bfloat16 [8192, 2048], P('ctx', 'head')
- key_grad: bfloat16 [8192, 2048], P('ctx', 'head')
- value_grad: bfloat16 [8192, 2048], P('ctx', 'head')
- conv_grad: float32 [3, 4, 2048], P(None, None, 'head')
- gain_grad: float32 [2048], P('head')
All inputs are finite; a program needn't handle non-finite values.
Results may differ from a plain program's by a relative error of at most 0.015.
Values may be sent and summed in bfloat16 or wider, within the bound.
A program may use at most 128 MiB of HBM per device.

v0:
```python
import jax
import jax.numpy as jnp
from jax import lax
from jax.sharding import PartitionSpec as P

HD = 128
TAPS = 4
GROUP = 512
D = 2048
norm_epsilon = 1e-05


def shifted(block, axis, distance):
    devices = range(lax.axis_size(axis))
    route = [(i - distance, i) for i in devices if i - distance in devices]
    return lax.ppermute(block, axis, route)


def prefix(value, axis, join, neutral):
    count = lax.axis_size(axis)
    place = lax.axis_index(axis)
    ahead = count - 1 - place
    gathered = jax.tree.map(
        lambda a, kind: lax.all_gather(a.astype(kind), axis), value, (jnp.bfloat16, jnp.bfloat16)
    )
    state = jax.tree.map(lambda a, e: jnp.zeros_like(a) + jnp.asarray(e, a.dtype), value, neutral)

    def one(turn, state):
        source = count - 1 - turn
        return join(
            state,
            jax.tree.map(
                lambda a, own: lax.dynamic_index_in_dim(a, source, 0, False).astype(own.dtype),
                gathered,
                value,
            ),
        )

    return lax.fori_loop(0, ahead, one, state)


def rounded(values):
    return values.astype(jnp.bfloat16)


def decay_tables(gate_blocks):
    running = jnp.cumsum(gate_blocks, axis=-1)
    closing = running[..., -1]
    gap_matrix = running[..., :, None] - running[..., None, :]
    block_size = gate_blocks.shape[-1]
    lower_mask = jnp.arange(block_size)[:, None] >= jnp.arange(block_size)[None, :]
    weights = jnp.where(lower_mask, jnp.exp(jnp.minimum(gap_matrix, 0.0)), 0.0)
    return (running, closing, weights)


def chain_step(earlier, later_part):
    return (
        earlier[0] + later_part[0],
        jnp.exp(later_part[0])[..., None, None] * earlier[1] + later_part[1],
    )


def local_chain(closing, blocks, backwards):

    def advance(partial_sum, block_item):
        return (chain_step(partial_sum, block_item), partial_sum)

    initial = (jnp.zeros(closing.shape[1:], jnp.float32), jnp.zeros(blocks.shape[1:], jnp.float32))
    return lax.scan(advance, initial, (closing, blocks), reverse=backwards)


def conv_forward(rim_rows, rows, weight, tok_here):
    extended = jnp.concatenate([rim_rows, rows], axis=0).astype(jnp.float32)
    result = weight[0][None, :] * extended[TAPS - 1 : TAPS - 1 + tok_here]
    for offset in range(1, TAPS):
        result = (
            result
            + weight[offset][None, :] * extended[TAPS - 1 - offset : TAPS - 1 - offset + tok_here]
        )
    return (rounded(result), extended)


def conv_backward(grad_rows, edge_rows, extended, weight, tok_here):
    ahead_all = jnp.concatenate([grad_rows, edge_rows], axis=0)
    input_grad = weight[0][None, :] * grad_rows
    weight_grad = [jnp.sum(grad_rows * extended[TAPS - 1 : TAPS - 1 + tok_here], axis=0)]
    for offset in range(1, TAPS):
        input_grad = input_grad + weight[offset][None, :] * ahead_all[offset : offset + tok_here]
        weight_grad.append(
            jnp.sum(grad_rows * extended[TAPS - 1 - offset : TAPS - 1 - offset + tok_here], axis=0)
        )
    return (rounded(input_grad), jnp.stack(weight_grad))


def body(query_rows, key_rows, value_rows, log_gate, conv_weight, norm_gain, mixed_grad):
    tok_here = query_rows.shape[0]
    width_here = query_rows.shape[1]
    heads_here = width_here // HD
    block_count = tok_here // GROUP
    rim_rows = shifted(
        jnp.stack(
            [
                query_rows[tok_here - (TAPS - 1) :],
                key_rows[tok_here - (TAPS - 1) :],
                value_rows[tok_here - (TAPS - 1) :],
            ]
        ),
        "ctx",
        1,
    )
    query_conv, query_ext = conv_forward(rim_rows[0], query_rows, conv_weight[0], tok_here)
    key_conv, key_ext = conv_forward(rim_rows[1], key_rows, conv_weight[1], tok_here)
    value_conv, value_ext = conv_forward(rim_rows[2], value_rows, conv_weight[2], tok_here)
    query_blocks = query_conv.reshape(block_count, GROUP, heads_here, HD)
    key_blocks = key_conv.reshape(block_count, GROUP, heads_here, HD)
    value_blocks = value_conv.reshape(block_count, GROUP, heads_here, HD)
    gate_blocks = log_gate.reshape(heads_here, block_count, GROUP).transpose(1, 0, 2)
    running, closing, weights = decay_tables(gate_blocks)
    grow_factor = jnp.exp(running).transpose(0, 2, 1)[..., None]
    shrink = jnp.exp(closing[..., None] - running).transpose(0, 2, 1)[..., None]
    scores = jnp.einsum(
        "nthd,nshd->nhts", query_blocks, key_blocks, preferred_element_type=jnp.float32
    )
    weights_low = rounded(scores * weights)
    key_scaled = rounded(key_blocks * shrink)
    blocks = jnp.einsum(
        "nshd,nshe->nhde", key_scaled, value_blocks, preferred_element_type=jnp.float32
    )
    device_sum, before = local_chain(closing, blocks, False)
    zero_state = jnp.zeros((heads_here, HD, HD), jnp.float32)
    all_totals = lax.all_gather(device_sum[0][None], "ctx", axis=0, tiled=True)
    device_index = lax.axis_index("ctx")
    cumulative = jnp.cumsum(all_totals, axis=0)
    before_me = cumulative[device_index] - all_totals[device_index]
    sources = jnp.arange(all_totals.shape[0])
    factor_table = jnp.where(
        (sources < device_index)[:, None],
        jnp.exp(jnp.minimum(before_me[None, :] - cumulative, 0.0)),
        0.0,
    )
    incoming = jnp.einsum(
        "nh,nhde->hde",
        factor_table,
        lax.all_gather(device_sum[1][None], "ctx", axis=0, tiled=True),
        precision=lax.Precision.HIGHEST,
    )
    group_in = jnp.exp(before[0])[..., None, None] * incoming[None] + before[1]
    state_low = rounded(group_in)
    attended = jnp.einsum(
        "nhts,nshe->nthe", weights_low, value_blocks, preferred_element_type=jnp.float32
    )
    attended = (
        attended
        + jnp.einsum("nthd,nhde->nthe", query_blocks, state_low, preferred_element_type=jnp.float32)
        * grow_factor
    )
    attended = attended.reshape(tok_here, width_here)
    grad_wide = mixed_grad.astype(jnp.float32)
    scaled = grad_wide * norm_gain[None, :]
    squares = lax.psum(jnp.sum(attended * attended, axis=1), "head")
    inverse = lax.rsqrt(squares / D + norm_epsilon)
    inner_sum = lax.psum(jnp.sum(scaled * attended, axis=1), "head") / D
    normed = attended * inverse[:, None]
    mixer_out = rounded(normed * norm_gain[None, :])
    gain_part = jnp.sum(grad_wide * normed, axis=0)
    out_grad = rounded(
        inverse[:, None] * (scaled - attended * (inverse * inverse * inner_sum)[:, None])
    )
    grad_blocks = out_grad.reshape(block_count, GROUP, heads_here, HD)
    grad_scores = rounded(
        jnp.einsum("nthe,nshe->nhts", grad_blocks, value_blocks, preferred_element_type=jnp.float32)
        * weights
    )
    query_scaled = rounded(query_blocks * grow_factor)
    back_blocks = jnp.einsum(
        "nthd,nthe->nhde", query_scaled, grad_blocks, preferred_element_type=jnp.float32
    )
    back_sum, back_before = local_chain(closing, back_blocks, True)
    later_state = prefix(
        (back_sum[0], back_sum[1]),
        "ctx",
        chain_step,
        (jnp.zeros((heads_here,), jnp.float32), zero_state),
    )[1]
    later_low = rounded(
        jnp.exp(back_before[0])[..., None, None] * later_state[None] + back_before[1]
    )
    query_cg = jnp.einsum(
        "nhts,nshd->nthd", grad_scores, key_blocks, preferred_element_type=jnp.float32
    )
    query_cg = (
        query_cg
        + jnp.einsum("nthe,nhde->nthd", grad_blocks, state_low, preferred_element_type=jnp.float32)
        * grow_factor
    )
    key_cg = jnp.einsum(
        "nhts,nthd->nshd", grad_scores, query_blocks, preferred_element_type=jnp.float32
    )
    key_cg = (
        key_cg
        + jnp.einsum("nshe,nhde->nshd", value_blocks, later_low, preferred_element_type=jnp.float32)
        * shrink
    )
    value_cg = jnp.einsum(
        "nhts,nthe->nshe", weights_low, grad_blocks, preferred_element_type=jnp.float32
    )
    value_cg = (
        value_cg
        + jnp.einsum("nshd,nhde->nshe", key_blocks, later_low, preferred_element_type=jnp.float32)
        * shrink
    )
    query_cg = query_cg.reshape(tok_here, width_here)
    key_cg = key_cg.reshape(tok_here, width_here)
    value_cg = value_cg.reshape(tok_here, width_here)
    edge_rows = shifted(
        jnp.stack([query_cg[: TAPS - 1], key_cg[: TAPS - 1], value_cg[: TAPS - 1]]), "ctx", -1
    )
    query_grad, query_taps = conv_backward(
        query_cg, edge_rows[0], query_ext, conv_weight[0], tok_here
    )
    key_grad, key_taps = conv_backward(key_cg, edge_rows[1], key_ext, conv_weight[1], tok_here)
    value_grad, value_taps = conv_backward(
        value_cg, edge_rows[2], value_ext, conv_weight[2], tok_here
    )
    conv_part = jnp.stack([query_taps, key_taps, value_taps])
    conv_grad, gain_grad = lax.psum((conv_part, gain_part), "ctx")
    return (mixer_out, query_grad, key_grad, value_grad, conv_grad, gain_grad)


def solution(mesh):
    placed = (
        P("ctx", "head"),
        P("ctx", "head"),
        P("ctx", "head"),
        P("head", "ctx"),
        P(None, None, "head"),
        P("head"),
        P("ctx", "head"),
    )
    return jax.shard_map(
        body,
        mesh=mesh,
        in_specs=placed,
        out_specs=(
            P("ctx", "head"),
            P("ctx", "head"),
            P("ctx", "head"),
            P("ctx", "head"),
            P(None, None, "head"),
            P("head"),
        ),
        check_vma=False,
    )
```

profile of v0, /device:TPU:0, one launch (start us, length us, event | category | flops | bytes accessed | tf_op | source)
XLA Modules:
  0.0 309.8 jit_solution(4000271757423066720)
XLA Ops:
  8.8 2.4 collective-permute-start
  11.2 2.2 reduce-window.6
  21.2 4.9 %fusion.49 = bf16[64,8,8,128]{3,2,1,0:T(8,128)(2,1)S(1)} fusion(f32[515,1024]{1,0:T(8,128)} %maximum_convert_fusion, f32[1024]{0:T(1024)S(1)} %bitcast.226, f32[1024]{0:T(1024)S(1)} %bitcast.228, f32[1024]{0:T(1024)S(1)} %bitcast.230, f32[1024]{0:T(1024)S(1)} %bitcast.224), kind=kLoop, calls=%fused_computation.94 | loop fusion | flops 4194304 | bytes 9453568
  28.5 22.8 %all-gather = f32[16,8,1]{1,2,0:T(1,128)S(1)} all-gather(f32[1,8,1]{1,2,0:T(1,128)S(1)} %get-tuple-element.187), channel_id=2, replica_groups=mesh['ctx'=16,'head'=2] {'ctx'}, dimensions={0}, use_global_device_ids=true | all-gather | bytes 544 | tf_op jit(solution)/shard_map/all_gather | solution.py:131
  58.5 2.3 copy.213
  62.0 2.9 multiply_convert_fusion.1
  65.0 2.0 copy-done.2
  66.9 2.8 fusion.42
  69.8 35.3 %all-gather.7.cloned.1.call-done = f32[128,128,128]{2,1,0:T(8,128)} async-done(((f32[8,128,128]{2,1,0:T(8,128)}), f32[128,128,128]{2,1,0:T(8,128)}) %all-gather.7.cloned.1.call-update) | async-done | bytes 8388624 | tf_op jit(solution)/shard_map/all_gather | solution.py:144
  105.1 12.5 %fusion = f32[8,1,128,128]{3,1,2,0:T(1,128)S(1)} fusion(f32[16,8,1,1]{0,2,3,1:T(1,128)S(1)} %copy.206, f32[16,8,128,128]{3,2,1,0:T(8,128)} %bitcast.188), kind=kOutput, calls=%fused_computation.2 | convolution fusion | flops 25165824 | bytes 8913408 | tf_op jit(solution)/shard_map/nh,nhde->hde/dot_general | solution.py:141
  119.5 5.1 %psum.28 = f32[512]{0:T(512)S(1)} all-reduce(f32[512]{0:T(512)S(1)} %get-tuple-element.206), channel_id=1, replica_groups=mesh['ctx'=16,'head'=2] {'head'}, use_global_device_ids=true, to_apply=%region_4.5 | all-reduce | flops 512 | bytes 4096 | tf_op jit(solution)/shard_map/psum | solution.py:160
  124.7 2.9 copy.169
  127.6 2.6 fusion.7
  130.2 4.9 %psum.29 = f32[512]{0:T(512)S(1)} all-reduce(f32[512]{0:T(512)S(1)} %get-tuple-element.166), channel_id=1, replica_groups=mesh['ctx'=16,'head'=2] {'head'}, use_global_device_ids=true, to_apply=%region_6.7 | all-reduce | flops 512 | bytes 4096 | tf_op jit(solution)/shard_map/psum | solution.py:162
  135.2 3.9 %fusion.6 = (bf16[512,1024]{1,0:T(8,128)(2,1)}, bf16[512,1024]{1,0:T(8,128)(2,1)}) fusion(bf16[512,1024]{1,0:T(8,128)(2,1)} %param.15, f32[512,1024]{1,0:T(8,128)} %copy.169, f32[512]{0:T(512)S(1)} %multiply_multiply_fusion, f32[1024]{0:T(1024)S(1)} %copy-done.25, f32[512]{0:T(512)S(1)} %add_rsqrt_fusion), kind=kLoop, calls=%fused_computation.19 | loop fusion | flops 4718592 | bytes 5251072 | tf_op jit(solution)/shard_map/convert_element_type | solution.py:43
  139.0 2.3 copy.214
  141.3 2.7 fusion.39
  144.0 18.6 %all-gather.3 = bf16[16,8,1]{1,2,0:T(2,128)(2,1)S(1)} all-gather(bf16[1,8,1]{1,2,0:T(2,128)(2,1)S(1)} %slice.396), channel_id=5, replica_groups=mesh['ctx'=16,'head'=2] {'ctx'}, dimensions={0}, use_global_device_ids=true | all-gather | bytes 272 | tf_op jit(solution)/shard_map/all_gather | solution.py:24
  162.7 4.0 %multiply_convert_fusion = bf16[8,512,512]{2,1,0:T(8,128)(2,1)S(1)} fusion(f32[8,512]{1,0:T(8,128)S(1)} %copy-done.27, pred[512,512]{1,0:T(8,128)(4,1)} %iota_compare_fusion, bf16[512,8,128]{0,2,1:T(8,128)(2,1)} %bitcast.185, bf16[64,8,8,128]{3,2,1,0:T(8,128)(2,1)S(1)} %fusion.49), kind=kOutput, calls=%fused_computation.4 | convolution fusion | flops 547356672 | bytes 6569984 | tf_op jit(solution)/shard_map/nthe,nshe->nhts/dot_general | solution.py:171
  173.1 4.4 %fusion.64 = f32[8,128,512]{2,1,0:T(8,128)} fusion(bf16[512,8,128]{0,2,1:T(8,128)(2,1)S(1)} %bitcast.187, bf16[8,512,512]{2,1,0:T(8,128)(2,1)} %copy-done.2), kind=kOutput, calls=%fused_computation.139 | convolution fusion | flops 536870912 | bytes 7340032 | tf_op jit(solution)/shard_map/nhts,nthe->nshe/dot_general | solution.py:204
  177.5 2.0 fusion.63
  179.6 13.5 %all-gather.9.cloned.1.call-done = bf16[128,128,128]{2,1,0:T(8,128)(2,1)} async-done(((bf16[8,128,128]{2,1,0:T(8,128)(2,1)}), bf16[128,128,128]{2,1,0:T(8,128)(2,1)}) %all-gather.9.cloned.1.call-update) | async-done | bytes 4194320 | tf_op jit(solution)/shard_map/all_gather | solution.py:24
  193.1 17.3 %while.9 = (s32[]{:T(128)}, f32[8,128,128]{2,1,0:T(8,128)S(1)}, s32[]{:T(128)}, bf16[16,8]{1,0:T(8,128)(2,1)S(1)}, bf16[16,8,128,128]{3,2,1,0:T(8,128)(2,1)}, /*index=5*/s32[]{:T(128)}, s32[]{:T(128)}, s32[]{:T(128)}, s32[]{:T(128)}) while((s32[]{:T(128)}, f32[8,128,128]{2,1,0:T(8,128)S(1)}, s32[]{:T(128)}, bf16[16,8]{1,0:T(8,128)(2,1)S(1)}, ...), condition=%wide.region_8.9_spmd, body=%wide.region_7.8_spmd.sunk | while | flops 393230 | bytes 1310955 | solution.py:39
  210.4 2.4 fusion.35
  214.4 2.4 fusion.36
  220.0 3.0 copy.176
  222.9 2.9 copy.192
  225.9 2.9 copy.190
  228.8 8.9 %multiply_reduce_fusion.3 = (f32[1024]{0:T(1024)S(1)}, f32[1024]{0:T(1024)S(1)}, f32[1024]{0:T(1024)S(1)}, f32[1024]{0:T(1024)S(1)}, bf16[512,1024]{1,0:T(8,128)(2,1)}) fusion(f32[512,1024]{1,0:T(8,128)} %copy.192, f32[515,1024]{1,0:T(8,128)} %maximum_convert_fusion, f32[3,1024]{1,0:T(4,128)S(1)} %get-tuple-element.188, f32[1024]{0:T(1024)S(1)} %bitcast.227, ...), kind=kLoop, calls=%fused_computation.62 | loop fusion | flops 9957376 | bytes 11579392 | tf_op jit(solution)/shard_map/reduce_sum | solution.py:86
  237.7 2.9 multiply_reduce_fusion.11
  240.6 2.9 multiply_reduce_fusion.7
  243.7 59.3 %all-reduce = (f32[3,4,1024]{2,1,0:T(4,128)}, f32[1024]{0:T(1024)}) all-reduce(f32[3,4,1024]{2,1,0:T(4,128)S(1)} %pad_maximum_fusion.4, f32[1024]{0:T(1024)S(1)} %get-tuple-element.165), channel_id=1, replica_groups=mesh['ctx'=16,'head'=2] {'ctx'}, use_global_device_ids=true, to_apply=%region_21.22 | all-reduce | flops 13312 | bytes 106496 | tf_op jit(solution)/shard_map/psum | solution.py:226
  (149 shorter events, 50.1 us)
Async XLA Ops:
  7.2 9.3 %copy-start.21 = (bf16[512,1024]{1,0:T(8,128)(2,1)S(1)}, bf16[512,1024]{1,0:T(8,128)(2,1)}, u32[]{:S(2)}) copy-start(bf16[512,1024]{1,0:T(8,128)(2,1)} %param.11) | copy-start | bytes 3145732
  7.2 97.9 %all-gather.7.cloned.1.call-start = ((), (), s32[]{:S(2)}) async-start(), calls=%async_computation | async-start | bytes 8912896 | tf_op jit(solution)/shard_map/all_gather | solution.py:144
  8.8 7.1 %collective-permute-start = (bf16[3,3,1024]{2,1,0:T(4,128)(2,1)S(1)}, bf16[3,3,1024]{2,1,0:T(4,128)(2,1)S(1)}, u32[]{:S(2)}, u32[]{:S(2)}) collective-permute-start(bf16[3,3,1024]{2,1,0:T(4,128)(2,1)S(1)} %pad_maximum_fusion.5), channel_id=1, source_target_pairs={{0,2},{2,4},{4,6},{6,8},{8,10},{10,12},{12,14},{14,16},{16,18},{18... | collective-permute-start | bytes 55304 | tf_op jit(solution)/shard_map/ppermute | solution.py:16
  13.6 2.1 copy-start.24
  15.7 2.5 copy-start.22
  15.8 10.3 %copy-start.28 = (f32[8]{0:T(128)}, f32[8]{0:T(128)S(1)}, u32[]{:S(2)}) copy-start(f32[8]{0:T(128)S(1)} %exponential_multiply_fusion) | copy-start | bytes 100
  21.2 4.9 %copy-start.18 = (bf16[512,8,128]{0,2,1:T(8,128)(2,1)S(1)}, bf16[512,8,128]{0,2,1:T(8,128)(2,1)}, u32[]{:S(2)}) copy-start(bf16[512,8,128]{0,2,1:T(8,128)(2,1)} %copy.163) | copy-start | bytes 3145732
  26.1 136.6 %copy-start.8 = (bf16[64,8,8,128]{3,2,1,0:T(8,128)(2,1)}, bf16[64,8,8,128]{3,2,1,0:T(8,128)(2,1)S(1)}, u32[]{:S(2)}) copy-start(bf16[64,8,8,128]{3,2,1,0:T(8,128)(2,1)S(1)} %fusion.49) | copy-start | bytes 3145732
  27.4 165.6 %all-gather.9.cloned.1.call-start = ((), (), s32[]{:S(2)}) async-start(), calls=%async_computation.1 | async-start | bytes 4456448 | tf_op jit(solution)/shard_map/all_gather | solution.py:24
  55.2 1.3 copy-start
  60.8 1.3 copy-start.26
  61.7 3.2 %copy-start.20 = (bf16[64,8,8,128]{3,2,1,0:T(8,128)(2,1)}, bf16[64,8,8,128]{3,2,1,0:T(8,128)(2,1)S(1)}, u32[]{:S(2)}) copy-start(bf16[64,8,8,128]{3,2,1,0:T(8,128)(2,1)S(1)} %fusion.78) | copy-start | bytes 3145732
  65.0 2.0 copy-start.2
  105.1 12.5 %copy-start.10 = (bf16[512,1024]{0,1:T(8,128)(2,1)S(1)}, bf16[512,1024]{0,1:T(8,128)(2,1)}, u32[]{:S(2)}) copy-start(bf16[512,1024]{0,1:T(8,128)(2,1)} %copy.213) | copy-start | bytes 3145732
  105.1 12.5 %copy-start.13 = (f32[8,128,512]{2,1,0:T(8,128)S(1)}, f32[8,128,512]{2,1,0:T(8,128)}, u32[]{:S(2)}) copy-start(f32[8,128,512]{2,1,0:T(8,128)} %fusion.42) | copy-start | bytes 6291460
  117.6 1.9 copy-start.16
  124.7 2.9 copy-start.25
  139.0 2.3 copy-start.29
  139.0 23.6 %copy-start.27 = (f32[8,512]{1,0:T(8,128)S(1)}, f32[8,512]{1,0:T(8,128)}, u32[]{:S(2)}) copy-start(f32[8,512]{1,0:T(8,128)} %bitcast_add_fusion) | copy-start | bytes 49156
  162.7 4.1 %copy-start.19 = (bf16[512,8,128]{0,2,1:T(8,128)(2,1)S(1)}, bf16[512,8,128]{0,2,1:T(8,128)(2,1)}, u32[]{:S(2)}) copy-start(bf16[512,8,128]{0,2,1:T(8,128)(2,1)} %copy.163) | copy-start | bytes 3145732
  166.7 2.3 copy-start.3
  166.7 2.3 copy-start.12
  166.7 2.5 copy-start.17
  169.7 1.3 copy-start.5
  173.1 4.4 %copy-start.4 = (bf16[8,512,512]{2,1,0:T(8,128)(2,1)S(1)}, bf16[8,512,512]{2,1,0:T(8,128)(2,1)}, u32[]{:S(2)}) copy-start(bf16[8,512,512]{2,1,0:T(8,128)(2,1)} %copy-done.3) | copy-start | bytes 12582916
  173.1 4.4 %copy-start.11 = (bf16[512,1024]{0,1:T(8,128)(2,1)S(1)}, bf16[512,1024]{0,1:T(8,128)(2,1)}, u32[]{:S(2)}) copy-start(bf16[512,1024]{0,1:T(8,128)(2,1)} %copy.213) | copy-start | bytes 3145732
  212.9 1.3 copy-start.6
  216.8 1.3 copy-start.7
  218.4 10.3 %collective-permute-start.1 = (f32[3,3,1024]{2,1,0:T(4,128)S(1)}, f32[3,3,1024]{2,1,0:T(4,128)S(1)}, u32[]{:S(2)}, u32[]{:S(2)}) collective-permute-start(f32[3,3,1024]{2,1,0:T(4,128)S(1)} %pad_maximum_fusion.3), channel_id=1, source_target_pairs={{2,0},{4,2},{6,4},{8,6},{10,8},{12,10},{14,12},{16,14},{18,16},{20... | collective-permute-start | bytes 110600 | tf_op jit(solution)/shard_map/ppermute | solution.py:16
  228.8 8.9 %copy-start.1 = (f32[515,1024]{1,0:T(8,128)S(1)}, f32[515,1024]{1,0:T(8,128)}, u32[]{:S(2)}) copy-start(f32[515,1024]{1,0:T(8,128)} %copy-done) | copy-start | bytes 6328324
  228.8 8.9 %copy-start.15 = (f32[512,1024]{1,0:T(8,128)S(1)}, f32[512,1024]{1,0:T(8,128)}, u32[]{:S(2)}) copy-start(f32[512,1024]{1,0:T(8,128)} %copy.176) | copy-start | bytes 6291460
  237.7 3.0 copy-start.14
  (2 other events, 2.5 us)
Sparse Core Ops, SparseCore 0:
  27.6 77.4 all-gather.6
  144.1 48.9 all-gather.8
where the time goes:
time: 311 us; the launch traced here: 310 us
  blocking collectives  111 us (36%)
  other arithmetic  55.7 us (18%)
  waiting for transfers between devices  48.9 us (16%)
  matrix products  41.3 us (13%)
  local copies, waits for them, and re-layouts  34.1 us (11%)
  between operations  14.5 us (5%)
  starting transfers between devices  3.99 us (1%)
    psum x1, blocking collectives, body(): conv_grad, gain_grad = lax.psum((conv_part, gain_part), 'ctx')  59.3 us
    all_gather x1, waiting for transfers between devices, body(): lax.all_gather(device_sum[1][None], 'ctx', axis=0, tiled=True)  35.3 us
    all_gather x1, blocking collectives, body(): all_totals = lax.all_gather(device_sum[0][None], 'ctx', axis=0, tiled=True)  22.8 us
    all_gather x1, blocking collectives, prefix(): lax.all_gather(a.astype(kind), axis)  18.6 us
    add x15, other arithmetic, chain_step(): jnp.exp(later_part[0])[..., None, None] * earlier[1] + later_part[1]  16.6 us
    reduce_sum x3, other arithmetic, conv_backward(): jnp.sum(grad_rows * extended[TAPS - 1:TAPS - 1 + tok_here], axis=0)  14.7 us
    all_gather x1, waiting for transfers between devices, prefix(): lax.all_gather(a.astype(kind), axis)  13.5 us
    dot_general x1, matrix products, body(): jnp.einsum('nh,nhde->hde', factor_table, lax.all_gather(device_sum[1][Non...  12.5 us
  transfers between devices with their start and end apart: 4, of which 2 were waited for; matrix products, arithmetic and copies ran while one was open for 14% of the time, Pallas kernels for 0%

commit v1 on v0

--- a/solution.py
+++ b/solution.py
@@ -128,7 +128,15 @@
     )
     device_sum, before = local_chain(closing, blocks, False)
     zero_state = jnp.zeros((heads_here, HD, HD), jnp.float32)
-    all_totals = lax.all_gather(device_sum[0][None], "ctx", axis=0, tiled=True)
+    block_2 = device_sum[0][None]
+    devices_2 = lax.axis_size("ctx")
+    hops = [(i_2, (i_2 + 1) % devices_2) for i_2 in range(devices_2)]
+    shards = [block_2]
+    for far in range(1, devices_2):
+        shards = [lax.ppermute(shards[0], "ctx", hops), *shards]
+    full = jnp.concatenate(shards, axis=0)
+    shift = (lax.axis_index("ctx") + 1) * shards[-1].shape[0]
+    all_totals = jnp.roll(full, shift, axis=0)
     device_index = lax.axis_index("ctx")
     cumulative = jnp.cumsum(all_totals, axis=0)
     before_me = cumulative[device_index] - all_totals[device_index]

time: 311 us -> 342 us (1.100)
  waiting for transfers between devices: 48.9 us -> 95.3 us
  blocking collectives: 111 us -> 87.1 us
    ppermute x0 -> x15, waiting for transfers between devices: none -> 80.7 us  [body(): shards = [lax.ppermute(shards[0], 'ctx', hops), *shards]]
    all_gather x1, waiting for transfers between devices: 35.3 us -> 0.01 us  [body(): lax.all_gather(device_sum[1][None], 'ctx', axis=0, tiled=True)]
    all_gather x1 -> x0, blocking collectives: 22.8 us -> none  [body(): all_totals = lax.all_gather(device_sum[0][None], 'ctx', axis=0, tiled=True)]
    unnamed x3 -> x4, other arithmetic: 6.81 us -> 7.99 us
    unnamed x61 -> x83, local copies, waits for them, and re-layouts: 8.88 us -> 9.28 us
  transfers between devices with their start and end apart: 4 -> 19, of which waited for: 2 -> 16; matrix products, arithmetic and copies ran while one was open for 14% -> 14% of each run, Pallas kernels for 0% -> 0%
where the time goes in v1:
time: 342 us; the launch traced here: 340 us
  waiting for transfers between devices  95.3 us (28%)
  blocking collectives  87.1 us (25%)
  other arithmetic  58.2 us (17%)
  matrix products  41.2 us (12%)
  local copies, waits for them, and re-layouts  36.6 us (11%)
  between operations  14.6 us (4%)
  starting transfers between devices  6.68 us (2%)
    ppermute x15, waiting for transfers between devices, body(): shards = [lax.ppermute(shards[0], 'ctx', hops), *shards]  80.7 us
    psum x1, blocking collectives, body(): conv_grad, gain_grad = lax.psum((conv_part, gain_part), 'ctx')  59.3 us
    all_gather x1, blocking collectives, prefix(): lax.all_gather(a.astype(kind), axis)  17 us
    add x15, other arithmetic, chain_step(): jnp.exp(later_part[0])[..., None, None] * earlier[1] + later_part[1]  16.6 us
    all_gather x1, waiting for transfers between devices, prefix(): lax.all_gather(a.astype(kind), axis)  14.6 us
    reduce_sum x3, other arithmetic, conv_backward(): jnp.sum(grad_rows * extended[TAPS - 1:TAPS - 1 + tok_here], axis=0)  14.4 us
    dot_general x1, matrix products, body(): jnp.einsum('nh,nhde->hde', factor_table, lax.all_gather(device_sum[1][Non...  12.5 us
    unnamed x83, local copies, waits for them, and re-layouts  9.28 us
  transfers between devices with their start and end apart: 19, of which 16 were waited for; matrix products, arithmetic and copies ran while one was open for 14% of the time, Pallas kernels for 0%

profile of v1, /device:TPU:0, one launch (start us, length us, event | category | flops | bytes accessed | tf_op | source)
XLA Modules:
  0.0 340.1 jit_solution(17409200392338837144)
XLA Ops:
  23.2 4.9 %fusion.49 = bf16[64,8,8,128]{3,2,1,0:T(8,128)(2,1)S(1)} fusion(f32[515,1024]{1,0:T(8,128)} %maximum_convert_fusion, f32[1024]{0:T(1024)S(1)} %bitcast.220, f32[1024]{0:T(1024)S(1)} %bitcast.222, f32[1024]{0:T(1024)S(1)} %bitcast.224, f32[1024]{0:T(1024)S(1)} %bitcast.218), kind=kLoop, calls=%fused_computation.94 | loop fusion | flops 4194304 | bytes 9453568
  35.4 5.7 %collective-permute-done.2 = f32[1,8]{1,0:T(1,128)S(1)} collective-permute-done((f32[1,8]{1,0:T(1,128)S(1)}, f32[1,8]{1,0:T(1,128)S(1)}, u32[]{:S(2)}, u32[]{:S(2)}) %collective-permute-start.2) | collective-permute-done | bytes 64 | tf_op jit(solution)/shard_map/ppermute | solution.py:136
  41.0 5.7 %collective-permute-done.3 = f32[1,8]{1,0:T(1,128)S(1)} collective-permute-done((f32[1,8]{1,0:T(1,128)S(1)}, f32[1,8]{1,0:T(1,128)S(1)}, u32[]{:S(2)}, u32[]{:S(2)}) %collective-permute-start.3) | collective-permute-done | bytes 64 | tf_op jit(solution)/shard_map/ppermute | solution.py:136
  46.7 5.7 %collective-permute-done.4 = f32[1,8]{1,0:T(1,128)S(1)} collective-permute-done((f32[1,8]{1,0:T(1,128)S(1)}, f32[1,8]{1,0:T(1,128)S(1)}, u32[]{:S(2)}, u32[]{:S(2)}) %collective-permute-start.4) | collective-permute-done | bytes 64 | tf_op jit(solution)/shard_map/ppermute | solution.py:136
  52.4 5.7 %collective-permute-done.5 = f32[1,8]{1,0:T(1,128)S(1)} collective-permute-done((f32[1,8]{1,0:T(1,128)S(1)}, f32[1,8]{1,0:T(1,128)S(1)}, u32[]{:S(2)}, u32[]{:S(2)}) %collective-permute-start.5) | collective-permute-done | bytes 64 | tf_op jit(solution)/shard_map/ppermute | solution.py:136
  58.1 5.7 %collective-permute-done.6 = f32[1,8]{1,0:T(1,128)S(1)} collective-permute-done((f32[1,8]{1,0:T(1,128)S(1)}, f32[1,8]{1,0:T(1,128)S(1)}, u32[]{:S(2)}, u32[]{:S(2)}) %collective-permute-start.6) | collective-permute-done | bytes 64 | tf_op jit(solution)/shard_map/ppermute | solution.py:136
  63.7 5.7 %collective-permute-done.7 = f32[1,8]{1,0:T(1,128)S(1)} collective-permute-done((f32[1,8]{1,0:T(1,128)S(1)}, f32[1,8]{1,0:T(1,128)S(1)}, u32[]{:S(2)}, u32[]{:S(2)}) %collective-permute-start.7) | collective-permute-done | bytes 64 | tf_op jit(solution)/shard_map/ppermute | solution.py:136
  69.4 5.7 %collective-permute-done.8 = f32[1,8]{1,0:T(1,128)S(1)} collective-permute-done((f32[1,8]{1,0:T(1,128)S(1)}, f32[1,8]{1,0:T(1,128)S(1)}, u32[]{:S(2)}, u32[]{:S(2)}) %collective-permute-start.8) | collective-permute-done | bytes 64 | tf_op jit(solution)/shard_map/ppermute | solution.py:136
  75.1 5.7 %collective-permute-done.9 = f32[1,8]{1,0:T(1,128)S(1)} collective-permute-done((f32[1,8]{1,0:T(1,128)S(1)}, f32[1,8]{1,0:T(1,128)S(1)}, u32[]{:S(2)}, u32[]{:S(2)}) %collective-permute-start.9) | collective-permute-done | bytes 64 | tf_op jit(solution)/shard_map/ppermute | solution.py:136
  80.7 5.7 %collective-permute-done.10 = f32[1,8]{1,0:T(1,128)S(1)} collective-permute-done((f32[1,8]{1,0:T(1,128)S(1)}, f32[1,8]{1,0:T(1,128)S(1)}, u32[]{:S(2)}, u32[]{:S(2)}) %collective-permute-start.10) | collective-permute-done | bytes 64 | tf_op jit(solution)/shard_map/ppermute | solution.py:136
  86.4 5.7 %collective-permute-done.11 = f32[1,8]{1,0:T(1,128)S(1)} collective-permute-done((f32[1,8]{1,0:T(1,128)S(1)}, f32[1,8]{1,0:T(1,128)S(1)}, u32[]{:S(2)}, u32[]{:S(2)}) %collective-permute-start.11) | collective-permute-done | bytes 64 | tf_op jit(solution)/shard_map/ppermute | solution.py:136
  92.1 5.7 %collective-permute-done.12 = f32[1,8]{1,0:T(1,128)S(1)} collective-permute-done((f32[1,8]{1,0:T(1,128)S(1)}, f32[1,8]{1,0:T(1,128)S(1)}, u32[]{:S(2)}, u32[]{:S(2)}) %collective-permute-start.12) | collective-permute-done | bytes 64 | tf_op jit(solution)/shard_map/ppermute | solution.py:136
  97.8 5.7 %collective-permute-done.13 = f32[1,8]{1,0:T(1,128)S(1)} collective-permute-done((f32[1,8]{1,0:T(1,128)S(1)}, f32[1,8]{1,0:T(1,128)S(1)}, u32[]{:S(2)}, u32[]{:S(2)}) %collective-permute-start.13) | collective-permute-done | bytes 64 | tf_op jit(solution)/shard_map/ppermute | solution.py:136
  103.4 5.7 %collective-permute-done.14 = f32[1,8]{1,0:T(1,128)S(1)} collective-permute-done((f32[1,8]{1,0:T(1,128)S(1)}, f32[1,8]{1,0:T(1,128)S(1)}, u32[]{:S(2)}, u32[]{:S(2)}) %collective-permute-start.14) | collective-permute-done | bytes 64 | tf_op jit(solution)/shard_map/ppermute | solution.py:136
  109.6 5.1 %collective-permute-done.15 = f32[1,8]{1,0:T(1,128)} collective-permute-done((f32[1,8]{1,0:T(1,128)S(1)}, f32[1,8]{1,0:T(1,128)}, u32[]{:S(2)}, u32[]{:S(2)}) %collective-permute-start.15) | collective-permute-done | bytes 64 | tf_op jit(solution)/shard_map/ppermute | solution.py:136
  127.9 2.9 multiply_convert_fusion.1
  135.7 12.5 %fusion = f32[8,1,128,128]{3,1,2,0:T(1,128)S(1)} fusion(f32[16,8,1,1]{0,2,3,1:T(1,128)S(1)} %copy.272, f32[16,8,128,128]{3,2,1,0:T(8,128)} %bitcast.189), kind=kOutput, calls=%fused_computation.2 | convolution fusion | flops 25165824 | bytes 8913408 | tf_op jit(solution)/shard_map/nh,nhde->hde/dot_general | solution.py:149
  150.1 5.8 %psum.28 = f32[512]{0:T(512)S(1)} all-reduce(f32[512]{0:T(512)S(1)} %get-tuple-element.211), channel_id=1, replica_groups=mesh['ctx'=16,'head'=2] {'head'}, use_global_device_ids=true, to_apply=%region_4.5 | all-reduce | flops 512 | bytes 4096 | tf_op jit(solution)/shard_map/psum | solution.py:168
  155.9 2.9 copy.235
  161.4 4.9 %psum.29 = f32[512]{0:T(512)S(1)} all-reduce(f32[512]{0:T(512)S(1)} %get-tuple-element.171), channel_id=1, replica_groups=mesh['ctx'=16,'head'=2] {'head'}, use_global_device_ids=true, to_apply=%region_6.7 | all-reduce | flops 512 | bytes 4096 | tf_op jit(solution)/shard_map/psum | solution.py:170
  166.4 3.9 %fusion.6 = (bf16[512,1024]{1,0:T(8,128)(2,1)}, bf16[512,1024]{1,0:T(8,128)(2,1)}) fusion(bf16[512,1024]{1,0:T(8,128)(2,1)} %param.15, f32[512,1024]{1,0:T(8,128)} %copy.235, f32[512]{0:T(512)S(1)} %multiply_multiply_fusion, f32[1024]{0:T(1024)S(1)} %copy-done.24, f32[512]{0:T(512)S(1)} %add_rsqrt_fusion), kind=kLoop, calls=%fused_computation.19 | loop fusion | flops 4718592 | bytes 5251072 | tf_op jit(solution)/shard_map/convert_element_type | solution.py:43
  175.2 17.0 %all-gather.2 = bf16[16,1,8]{2,1,0:T(2,128)(2,1)S(1)} all-gather(bf16[1,1,8]{2,1,0:T(2,128)(2,1)S(1)} %copy-done.38), channel_id=1, replica_groups=mesh['ctx'=16,'head'=2] {'ctx'}, dimensions={0}, use_global_device_ids=true | all-gather | bytes 272 | tf_op jit(solution)/shard_map/all_gather | solution.py:24
  192.3 4.0 %multiply_convert_fusion = bf16[8,512,512]{2,1,0:T(8,128)(2,1)S(1)} fusion(f32[8,512]{1,0:T(8,128)} %bitcast_add_fusion.1, pred[512,512]{1,0:T(8,128)(4,1)S(1)} %iota_compare_fusion, bf16[512,8,128]{0,2,1:T(8,128)(2,1)} %bitcast.186, bf16[64,8,8,128]{3,2,1,0:T(8,128)(2,1)S(1)} %fusion.49), kind=kOutput, calls=%fused_computation.4 | convolution fusion | flops 547356672 | bytes 6569984 | tf_op jit(solution)/shard_map/nthe,nshe->nhts/dot_general | solution.py:179
  202.7 4.4 %fusion.65 = f32[8,128,512]{2,1,0:T(8,128)} fusion(bf16[512,8,128]{0,2,1:T(8,128)(2,1)S(1)} %bitcast.188, bf16[8,512,512]{2,1,0:T(8,128)(2,1)} %copy-done.2), kind=kOutput, calls=%fused_computation.142 | convolution fusion | flops 536870912 | bytes 7340032 | tf_op jit(solution)/shard_map/nhts,nthe->nshe/dot_general | solution.py:212
  209.1 14.6 %all-gather.8.cloned.1.call-done = bf16[128,128,128]{2,1,0:T(8,128)(2,1)} async-done(((bf16[8,128,128]{2,1,0:T(8,128)(2,1)}), bf16[128,128,128]{2,1,0:T(8,128)(2,1)}) %all-gather.8.cloned.1.call-update) | async-done | bytes 4194320 | tf_op jit(solution)/shard_map/all_gather | solution.py:24
  223.8 17.3 %while.9 = (s32[]{:T(128)}, f32[8,128,128]{2,1,0:T(8,128)S(1)}, s32[]{:T(128)}, bf16[16,8]{1,0:T(8,128)(2,1)S(1)}, bf16[16,8,128,128]{3,2,1,0:T(8,128)(2,1)}, /*index=5*/s32[]{:T(128)}, s32[]{:T(128)}, s32[]{:T(128)}, s32[]{:T(128)}) while((s32[]{:T(128)}, f32[8,128,128]{2,1,0:T(8,128)S(1)}, s32[]{:T(128)}, bf16[16,8]{1,0:T(8,128)(2,1)S(1)}, ...), condition=%wide.region_8.9_spmd, body=%wide.region_7.8_spmd.sunk | while | flops 393230 | bytes 1310955 | solution.py:39
  250.7 2.9 copy.242
  253.6 2.9 copy.258
  256.5 2.9 copy.256
  259.5 8.5 %multiply_reduce_fusion.3 = (f32[1024]{0:T(1024)S(1)}, f32[1024]{0:T(1024)S(1)}, f32[1024]{0:T(1024)S(1)}, f32[1024]{0:T(1024)S(1)}, bf16[512,1024]{1,0:T(8,128)(2,1)}) fusion(f32[512,1024]{1,0:T(8,128)} %copy.258, f32[515,1024]{1,0:T(8,128)} %maximum_convert_fusion, f32[3,1024]{1,0:T(4,128)S(1)} %get-tuple-element.191, f32[1024]{0:T(1024)S(1)} %bitcast.221, ...), kind=kLoop, calls=%fused_computation.62 | loop fusion | flops 9957376 | bytes 11579392 | tf_op jit(solution)/shard_map/reduce_sum | solution.py:86
  268.0 2.9 multiply_reduce_fusion.11
  274.0 59.3 %all-reduce = (f32[3,4,1024]{2,1,0:T(4,128)}, f32[1024]{0:T(1024)}) all-reduce(f32[3,4,1024]{2,1,0:T(4,128)S(1)} %pad_maximum_fusion.4, f32[1024]{0:T(1024)S(1)} %get-tuple-element.170), channel_id=1, replica_groups=mesh['ctx'=16,'head'=2] {'ctx'}, use_global_device_ids=true, to_apply=%region_21.22 | all-reduce | flops 13312 | bytes 106496 | tf_op jit(solution)/shard_map/psum | solution.py:234
  (196 shorter events, 88.9 us)
Async XLA Ops:
  7.2 13.0 %copy-start.21 = (bf16[512,1024]{1,0:T(8,128)(2,1)S(1)}, bf16[512,1024]{1,0:T(8,128)(2,1)}, u32[]{:S(2)}) copy-start(bf16[512,1024]{1,0:T(8,128)(2,1)} %param.10) | copy-start | bytes 3145732
  7.2 128.5 %all-gather.6.cloned.1.call-start = ((), (), s32[]{:S(2)}) async-start(), calls=%async_computation | async-start | bytes 8912896 | tf_op jit(solution)/shard_map/all_gather | solution.py:152
  8.8 8.5 %collective-permute-start = (bf16[3,3,1024]{2,1,0:T(4,128)(2,1)S(1)}, bf16[3,3,1024]{2,1,0:T(4,128)(2,1)S(1)}, u32[]{:S(2)}, u32[]{:S(2)}) collective-permute-start(bf16[3,3,1024]{2,1,0:T(4,128)(2,1)S(1)} %pad_maximum_fusion.5), channel_id=1, source_target_pairs={{0,2},{2,4},{4,6},{6,8},{8,10},{10,12},{12,14},{14,16},{16,18},{18... | collective-permute-start | bytes 55304 | tf_op jit(solution)/shard_map/ppermute | solution.py:16
  28.1 164.2 %copy-start.8 = (bf16[64,8,8,128]{3,2,1,0:T(8,128)(2,1)}, bf16[64,8,8,128]{3,2,1,0:T(8,128)(2,1)S(1)}, u32[]{:S(2)}) copy-start(bf16[64,8,8,128]{3,2,1,0:T(8,128)(2,1)S(1)} %fusion.49) | copy-start | bytes 3145732
  29.5 194.3 %all-gather.8.cloned.1.call-start = ((), (), s32[]{:S(2)}) async-start(), calls=%async_computation.1 | async-start | bytes 4456448 | tf_op jit(solution)/shard_map/all_gather | solution.py:24
  29.5 5.8 %collective-permute-start.1 = (f32[1,8]{1,0:T(1,128)}, f32[1,8]{1,0:T(1,128)S(1)}, u32[]{:S(2)}, u32[]{:S(2)}) collective-permute-start(f32[1,8]{1,0:T(1,128)} %bitcast.92), channel_id=1, source_target_pairs={{0,2},{2,4},{4,6},{6,8},{8,10},{10,12},{12,14},{14,16},{16,18},{18... | collective-permute-start | bytes 104 | tf_op jit(solution)/shard_map/ppermute | solution.py:136
  35.4 5.7 %collective-permute-start.2 = (f32[1,8]{1,0:T(1,128)S(1)}, f32[1,8]{1,0:T(1,128)S(1)}, u32[]{:S(2)}, u32[]{:S(2)}) collective-permute-start(f32[1,8]{1,0:T(1,128)S(1)} %collective-permute-done.1), channel_id=1, source_target_pairs={{0,2},{2,4},{4,6},{6,8},{8,10},{10,12},{12,14},{14,16},{16,18},{18... | collective-permute-start | bytes 104 | tf_op jit(solution)/shard_map/ppermute | solution.py:136
  41.0 5.7 %collective-permute-start.3 = (f32[1,8]{1,0:T(1,128)S(1)}, f32[1,8]{1,0:T(1,128)S(1)}, u32[]{:S(2)}, u32[]{:S(2)}) collective-permute-start(f32[1,8]{1,0:T(1,128)S(1)} %collective-permute-done.2), channel_id=1, source_target_pairs={{0,2},{2,4},{4,6},{6,8},{8,10},{10,12},{12,14},{14,16},{16,18},{18... | collective-permute-start | bytes 104 | tf_op jit(solution)/shard_map/ppermute | solution.py:136
  46.7 62.4 %copy-start.26 = (f32[1,8]{1,0:T(1,128)}, f32[1,8]{1,0:T(1,128)S(1)}, u32[]{:S(2)}) copy-start(f32[1,8]{1,0:T(1,128)S(1)} %collective-permute-done.3) | copy-start | bytes 100
  46.7 5.7 %collective-permute-start.4 = (f32[1,8]{1,0:T(1,128)S(1)}, f32[1,8]{1,0:T(1,128)S(1)}, u32[]{:S(2)}, u32[]{:S(2)}) collective-permute-start(f32[1,8]{1,0:T(1,128)S(1)} %collective-permute-done.3), channel_id=1, source_target_pairs={{0,2},{2,4},{4,6},{6,8},{8,10},{10,12},{12,14},{14,16},{16,18},{18... | collective-permute-start | bytes 104 | tf_op jit(solution)/shard_map/ppermute | solution.py:136
  52.4 56.7 %copy-start.27 = (f32[1,8]{1,0:T(1,128)}, f32[1,8]{1,0:T(1,128)S(1)}, u32[]{:S(2)}) copy-start(f32[1,8]{1,0:T(1,128)S(1)} %collective-permute-done.4) | copy-start | bytes 100
  52.4 5.7 %collective-permute-start.5 = (f32[1,8]{1,0:T(1,128)S(1)}, f32[1,8]{1,0:T(1,128)S(1)}, u32[]{:S(2)}, u32[]{:S(2)}) collective-permute-start(f32[1,8]{1,0:T(1,128)S(1)} %collective-permute-done.4), channel_id=1, source_target_pairs={{0,2},{2,4},{4,6},{6,8},{8,10},{10,12},{12,14},{14,16},{16,18},{18... | collective-permute-start | bytes 104 | tf_op jit(solution)/shard_map/ppermute | solution.py:136
  58.1 51.1 %copy-start.28 = (f32[1,8]{1,0:T(1,128)}, f32[1,8]{1,0:T(1,128)S(1)}, u32[]{:S(2)}) copy-start(f32[1,8]{1,0:T(1,128)S(1)} %collective-permute-done.5) | copy-start | bytes 100
  58.1 5.7 %collective-permute-start.6 = (f32[1,8]{1,0:T(1,128)S(1)}, f32[1,8]{1,0:T(1,128)S(1)}, u32[]{:S(2)}, u32[]{:S(2)}) collective-permute-start(f32[1,8]{1,0:T(1,128)S(1)} %collective-permute-done.5), channel_id=1, source_target_pairs={{0,2},{2,4},{4,6},{6,8},{8,10},{10,12},{12,14},{14,16},{16,18},{18... | collective-permute-start | bytes 104 | tf_op jit(solution)/shard_map/ppermute | solution.py:136
  63.7 45.4 %copy-start.29 = (f32[1,8]{1,0:T(1,128)}, f32[1,8]{1,0:T(1,128)S(1)}, u32[]{:S(2)}) copy-start(f32[1,8]{1,0:T(1,128)S(1)} %collective-permute-done.6) | copy-start | bytes 100
  63.7 5.7 %collective-permute-start.7 = (f32[1,8]{1,0:T(1,128)S(1)}, f32[1,8]{1,0:T(1,128)S(1)}, u32[]{:S(2)}, u32[]{:S(2)}) collective-permute-start(f32[1,8]{1,0:T(1,128)S(1)} %collective-permute-done.6), channel_id=1, source_target_pairs={{0,2},{2,4},{4,6},{6,8},{8,10},{10,12},{12,14},{14,16},{16,18},{18... | collective-permute-start | bytes 104 | tf_op jit(solution)/shard_map/ppermute | solution.py:136
  69.4 39.7 %copy-start.30 = (f32[1,8]{1,0:T(1,128)}, f32[1,8]{1,0:T(1,128)S(1)}, u32[]{:S(2)}) copy-start(f32[1,8]{1,0:T(1,128)S(1)} %collective-permute-done.7) | copy-start | bytes 100
  69.4 5.7 %collective-permute-start.8 = (f32[1,8]{1,0:T(1,128)S(1)}, f32[1,8]{1,0:T(1,128)S(1)}, u32[]{:S(2)}, u32[]{:S(2)}) collective-permute-start(f32[1,8]{1,0:T(1,128)S(1)} %collective-permute-done.7), channel_id=1, source_target_pairs={{0,2},{2,4},{4,6},{6,8},{8,10},{10,12},{12,14},{14,16},{16,18},{18... | collective-permute-start | bytes 104 | tf_op jit(solution)/shard_map/ppermute | solution.py:136
  75.1 34.1 %copy-start.31 = (f32[1,8]{1,0:T(1,128)}, f32[1,8]{1,0:T(1,128)S(1)}, u32[]{:S(2)}) copy-start(f32[1,8]{1,0:T(1,128)S(1)} %collective-permute-done.8) | copy-start | bytes 100
  75.1 5.7 %collective-permute-start.9 = (f32[1,8]{1,0:T(1,128)S(1)}, f32[1,8]{1,0:T(1,128)S(1)}, u32[]{:S(2)}, u32[]{:S(2)}) collective-permute-start(f32[1,8]{1,0:T(1,128)S(1)} %collective-permute-done.8), channel_id=1, source_target_pairs={{0,2},{2,4},{4,6},{6,8},{8,10},{10,12},{12,14},{14,16},{16,18},{18... | collective-permute-start | bytes 104 | tf_op jit(solution)/shard_map/ppermute | solution.py:136
  80.7 28.4 %copy-start.32 = (f32[1,8]{1,0:T(1,128)}, f32[1,8]{1,0:T(1,128)S(1)}, u32[]{:S(2)}) copy-start(f32[1,8]{1,0:T(1,128)S(1)} %collective-permute-done.9) | copy-start | bytes 100
  80.7 5.7 %collective-permute-start.10 = (f32[1,8]{1,0:T(1,128)S(1)}, f32[1,8]{1,0:T(1,128)S(1)}, u32[]{:S(2)}, u32[]{:S(2)}) collective-permute-start(f32[1,8]{1,0:T(1,128)S(1)} %collective-permute-done.9), channel_id=1, source_target_pairs={{0,2},{2,4},{4,6},{6,8},{8,10},{10,12},{12,14},{14,16},{16,18},{18... | collective-permute-start | bytes 104 | tf_op jit(solution)/shard_map/ppermute | solution.py:136
  86.4 22.8 %copy-start.33 = (f32[1,8]{1,0:T(1,128)}, f32[1,8]{1,0:T(1,128)S(1)}, u32[]{:S(2)}) copy-start(f32[1,8]{1,0:T(1,128)S(1)} %collective-permute-done.10) | copy-start | bytes 100
  86.4 5.7 %collective-permute-start.11 = (f32[1,8]{1,0:T(1,128)S(1)}, f32[1,8]{1,0:T(1,128)S(1)}, u32[]{:S(2)}, u32[]{:S(2)}) collective-permute-start(f32[1,8]{1,0:T(1,128)S(1)} %collective-permute-done.10), channel_id=1, source_target_pairs={{0,2},{2,4},{4,6},{6,8},{8,10},{10,12},{12,14},{14,16},{16,18},{18... | collective-permute-start | bytes 104 | tf_op jit(solution)/shard_map/ppermute | solution.py:136
  92.1 17.1 %copy-start.34 = (f32[1,8]{1,0:T(1,128)}, f32[1,8]{1,0:T(1,128)S(1)}, u32[]{:S(2)}) copy-start(f32[1,8]{1,0:T(1,128)S(1)} %collective-permute-done.11) | copy-start | bytes 100
  92.1 5.7 %collective-permute-start.12 = (f32[1,8]{1,0:T(1,128)S(1)}, f32[1,8]{1,0:T(1,128)S(1)}, u32[]{:S(2)}, u32[]{:S(2)}) collective-permute-start(f32[1,8]{1,0:T(1,128)S(1)} %collective-permute-done.11), channel_id=1, source_target_pairs={{0,2},{2,4},{4,6},{6,8},{8,10},{10,12},{12,14},{14,16},{16,18},{18... | collective-permute-start | bytes 104 | tf_op jit(solution)/shard_map/ppermute | solution.py:136
  97.8 5.7 %collective-permute-start.13 = (f32[1,8]{1,0:T(1,128)S(1)}, f32[1,8]{1,0:T(1,128)S(1)}, u32[]{:S(2)}, u32[]{:S(2)}) collective-permute-start(f32[1,8]{1,0:T(1,128)S(1)} %collective-permute-done.12), channel_id=1, source_target_pairs={{0,2},{2,4},{4,6},{6,8},{8,10},{10,12},{12,14},{14,16},{16,18},{18... | collective-permute-start | bytes 104 | tf_op jit(solution)/shard_map/ppermute | solution.py:136
  103.4 5.7 %collective-permute-start.14 = (f32[1,8]{1,0:T(1,128)S(1)}, f32[1,8]{1,0:T(1,128)S(1)}, u32[]{:S(2)}, u32[]{:S(2)}) collective-permute-start(f32[1,8]{1,0:T(1,128)S(1)} %collective-permute-done.13), channel_id=1, source_target_pairs={{0,2},{2,4},{4,6},{6,8},{8,10},{10,12},{12,14},{14,16},{16,18},{18... | collective-permute-start | bytes 104 | tf_op jit(solution)/shard_map/ppermute | solution.py:136
  109.1 5.6 %collective-permute-start.15 = (f32[1,8]{1,0:T(1,128)S(1)}, f32[1,8]{1,0:T(1,128)}, u32[]{:S(2)}, u32[]{:S(2)}) collective-permute-start(f32[1,8]{1,0:T(1,128)S(1)} %collective-permute-done.14), channel_id=1, source_target_pairs={{0,2},{2,4},{4,6},{6,8},{8,10},{10,12},{12,14},{14,16},{16,18},{18... | collective-permute-start | bytes 104 | tf_op jit(solution)/shard_map/ppermute | solution.py:136
  135.7 12.5 %copy-start.10 = (bf16[512,1024]{0,1:T(8,128)(2,1)S(1)}, bf16[512,1024]{0,1:T(8,128)(2,1)}, u32[]{:S(2)}) copy-start(bf16[512,1024]{0,1:T(8,128)(2,1)} %copy.278) | copy-start | bytes 3145732
  135.7 12.5 %copy-start.13 = (f32[8,128,512]{2,1,0:T(8,128)S(1)}, f32[8,128,512]{2,1,0:T(8,128)}, u32[]{:S(2)}) copy-start(f32[8,128,512]{2,1,0:T(8,128)} %fusion.42) | copy-start | bytes 6291460
  249.1 10.3 %collective-permute-start.16 = (f32[3,3,1024]{2,1,0:T(4,128)S(1)}, f32[3,3,1024]{2,1,0:T(4,128)S(1)}, u32[]{:S(2)}, u32[]{:S(2)}) collective-permute-start(f32[3,3,1024]{2,1,0:T(4,128)S(1)} %pad_maximum_fusion.3), channel_id=1, source_target_pairs={{2,0},{4,2},{6,4},{8,6},{10,8},{12,10},{14,12},{16,14},{18,16},{20... | collective-permute-start | bytes 110600 | tf_op jit(solution)/shard_map/ppermute | solution.py:16
  (28 other events, 109.4 us)
Sparse Core Ops, SparseCore 0:
  29.6 77.5 all-gather.5
  175.3 48.3 all-gather.7
